TPU v7x, 512 devices: a whole 4x4x16 slice. The times are simulated.
512 devices in a mesh: seq: 64 (over y_lo, z, core), tensor: 8 (over x, y_hi).
Axes of the slice: x: 4, y: 4 (y_hi: 2, y_lo: 2; y = y_hi * 2 + y_lo), z: 16, core: 2. Of those that a mesh axis runs over, the one named last changes fastest.
Arguments:
- trunk: bfloat16 [2, 4096, 1536], P(None, 'seq', 'tensor'), may hold values from -12 to 12
- w_out: bfloat16 [1536, 1536], P('tensor', 'seq'), may hold values from -1 to 1
- gain_coarse: float32 [1536], replicated, may hold values from 0.1 to 1.9
- w_conv1: bfloat16 [5, 1536, 1536], P(None, 'seq', 'tensor'), may hold values from -0.0625 to 0.0625
- w_up: bfloat16 [1536, 2, 768], P('seq', None, 'tensor'), may hold values from -0.15625 to 0.15625
- skip: bfloat16 [2, 8192, 768], P(None, 'seq', 'tensor'), may hold values from -12 to 12
- gain_fine: float32 [768], replicated, may hold values from 0.1 to 1.9
- w_conv2: bfloat16 [5, 768, 768], P(None, 'seq', 'tensor'), may hold values from -0.09375 to 0.09375
- cotangent: bfloat16 [2, 8192, 768], P(None, 'seq', 'tensor'), may hold values from -6 to 6
Outputs:
- decoded: bfloat16 [2, 8192, 768], P(None, 'seq', 'tensor')
- skip_grad: bfloat16 [2, 8192, 768], P(None, 'seq', 'tensor')
- trunk_grad: bfloat16 [2, 4096, 1536], P(None, 'seq', 'tensor')
All inputs are finite; a program needn't handle non-finite values.
Results may differ from a plain program's by a relative error of at most 0.02.
Values may be sent and summed in bfloat16 or wider, within the bound.
No kernel may reach another device: no remote copies, remote signals or barrier semaphores. Data moves between devices by JAX's collectives and lax.ppermute only.
A program may use at most 64 MiB of HBM per device.

v0:
```python
import jax
import jax.numpy as jnp
from jax import lax
from jax.sharding import PartitionSpec as P

C_COARSE = 1536
C_FINE = 768
EPS = 1e-06


def extended(shard, sides, width):
    for axis, dim in sides:
        size, length = (lax.axis_size(axis), shard.shape[dim])
        up = [(i, (i + 1) % size) for i in range(size - 1)]
        down = [(j, i) for i, j in up]
        last = lax.slice_in_dim(shard, length - width, length, axis=dim)
        leading = lax.slice_in_dim(shard, 0, width, axis=dim)
        before = lax.ppermute(last, axis, up)
        after = lax.ppermute(leading, axis, down)
        shard = jnp.concatenate([before, shard, after], axis=dim)
    return shard


def matmul(left, right):
    return lax.dot_general(
        left, right, (((left.ndim - 1,), (0,)), ((), ())), preferred_element_type=jnp.float32
    )


def matmul_back(left, right):
    return lax.dot_general(
        left,
        right,
        (((left.ndim - 1,), (right.ndim - 1,)), ((), ())),
        preferred_element_type=jnp.float32,
    )


def activate(field, gain):
    scaled = field * lax.rsqrt(jnp.mean(field * field, axis=-1, keepdims=True) + EPS)
    return jax.nn.gelu(scaled * gain)


def widen(field):
    return extended(field, (("seq", 1),), 2)


def spread(field):
    return lax.all_gather(field, "tensor", axis=2, tiled=True)


def conv_rows(total, wide, piece):
    length = wide.shape[1] - 4
    for k in range(5):
        total = total + matmul(wide[:, k : k + length], piece[k])
    return total


def conv_back(wide_grad, piece):
    length = wide_grad.shape[1] - 4
    total = jnp.zeros((wide_grad.shape[0], length, piece.shape[1]), jnp.float32)
    for k in range(5):
        total = total + matmul_back(wide_grad[:, 4 - k : 4 - k + length], piece[k])
    return total


def norm_back(partial_grad, field_full, gain, rank, part):
    field = field_full.astype(jnp.float32)
    start = rank * part
    whole = lax.psum(partial_grad.astype(jnp.bfloat16), "tensor").astype(jnp.float32)

    def apply(value):
        return activate(value, gain)

    _, pull = jax.vjp(apply, field)
    return lax.dynamic_slice_in_dim(pull(whole)[0], start, part, 2)


def per_device(trunk, w_out, gain_coarse, w_conv1, w_up, skip, gain_fine, w_conv2, cotangent):
    rank = lax.axis_index("tensor")
    part_coarse = C_COARSE // lax.axis_size("tensor")
    part_fine = C_FINE // lax.axis_size("tensor")
    seqs = trunk.shape[0]
    slab = trunk.shape[1]
    out_w, up_w, conv2_w = (
        lax.all_gather(w_out, "seq", axis=1, tiled=True),
        lax.all_gather(w_up, "seq", axis=0, tiled=True),
        lax.all_gather(w_conv2, "seq", axis=1, tiled=True),
    )
    partial_proj = matmul(trunk, out_w)
    projected = lax.psum_scatter(
        partial_proj.astype(jnp.bfloat16), "tensor", scatter_dimension=2, tiled=True
    )
    projected_full = lax.all_gather(projected, "tensor", axis=2, tiled=True)
    act_coarse = activate(projected_full.astype(jnp.float32), gain_coarse).astype(jnp.bfloat16)
    coarse_wide = widen(act_coarse)
    empty_coarse = jnp.zeros((seqs, slab, part_coarse), jnp.float32)
    mixed_coarse = conv_rows(
        empty_coarse, coarse_wide, lax.all_gather(w_conv1, "seq", axis=1, tiled=True)
    )
    lifted = (projected.astype(jnp.float32) + mixed_coarse).astype(jnp.bfloat16)
    lifted_full = spread(lifted)
    upper = matmul(lifted_full, up_w).reshape(seqs, 2 * slab, part_fine)
    merged = (upper + skip.astype(jnp.float32)).astype(jnp.bfloat16)
    merged_full = spread(merged)
    act_fine = activate(merged_full.astype(jnp.float32), gain_fine).astype(jnp.bfloat16)
    fine_wide = widen(act_fine)
    empty_fine = jnp.zeros((seqs, 2 * slab, part_fine), jnp.float32)
    mixed_fine = conv_rows(empty_fine, fine_wide, conv2_w)
    decoded = (merged.astype(jnp.float32) + mixed_fine).astype(jnp.bfloat16)
    cot_wide = widen(cotangent)
    back_fine = conv_back(cot_wide, conv2_w)
    skip_grad = (
        cotangent.astype(jnp.float32)
        + norm_back(back_fine, merged_full, gain_fine, rank, part_fine)
    ).astype(jnp.bfloat16)
    folded = skip_grad.reshape(seqs, slab, 2 * part_fine)
    up_partial = matmul_back(folded, up_w.reshape(up_w.shape[0], 2 * part_fine))
    lifted_grad = lax.psum_scatter(
        up_partial.astype(jnp.bfloat16), "tensor", scatter_dimension=2, tiled=True
    )
    grad_wide = widen(lifted_grad)
    back_coarse = conv_back(grad_wide, lax.all_gather(w_conv1, "seq", axis=1, tiled=True))
    projected_grad = (
        lifted_grad.astype(jnp.float32)
        + norm_back(back_coarse, projected_full, gain_coarse, rank, part_coarse)
    ).astype(jnp.bfloat16)
    grad_full = spread(projected_grad)
    trunk_grad = matmul_back(grad_full, out_w).astype(jnp.bfloat16)
    return (decoded, skip_grad, trunk_grad)


def solution(mesh):
    in_specs = (
        P(None, "seq", "tensor"),
        P("tensor", "seq"),
        P(),
        P(None, "seq", "tensor"),
        P("seq", None, "tensor"),
        P(None, "seq", "tensor"),
        P(),
        P(None, "seq", "tensor"),
        P(None, "seq", "tensor"),
    )
    out_specs = (P(None, "seq", "tensor"), P(None, "seq", "tensor"), P(None, "seq", "tensor"))
    return jax.shard_map(
        per_device, mesh=mesh, in_specs=in_specs, out_specs=out_specs, check_vma=False
    )
```

profile of v0, /device:TPU:32, one launch (start us, length us, event | category | flops | bytes accessed | tf_op | source)
XLA Modules:
  0.0 605.8 jit_solution(13952073995251404903)
XLA Ops:
  8.1 69.1 %all_gather.25 = bf16[192,1536]{0,1:T(8,128)(2,1)S(1)} all-gather(bf16[192,24]{0,1:T(8,128)(2,1)} %param.10), channel_id=1, replica_groups=mesh['seq'=64,'tensor'=8] {'seq'}, dimensions={1}, use_global_device_ids=true | all-gather | bytes 599040 | tf_op jit(solution)/shard_map/all_gather | solution.py:86
  78.1 1.1 reshape.66
  80.6 5.0 collective-permute-start.4
  85.6 1.9 collective-permute-start.5
  88.9 65.4 %all_gather.31 = bf16[5,768,96]{2,0,1:T(8,128)(2,1)S(1)} all-gather(bf16[5,12,96]{2,0,1:T(8,128)(2,1)S(1)} %copy.52), channel_id=1, replica_groups=mesh['seq'=64,'tensor'=8] {'seq'}, dimensions={1}, use_global_device_ids=true | all-gather | bytes 748800 | tf_op jit(solution)/shard_map/all_gather | solution.py:88
  154.3 1.4 fusion.107
  155.8 0.9 copy.76
  157.0 0.9 copy.75
  158.8 0.9 copy.78
  160.6 62.1 %all_gather.29 = bf16[1536,2,96]{2,0,1:T(8,128)(2,1)S(1)} all-gather(bf16[24,2,96]{2,0,1:T(8,128)(2,1)} %copy.46), channel_id=1, replica_groups=mesh['seq'=64,'tensor'=8] {'seq'}, dimensions={0}, use_global_device_ids=true | all-gather | bytes 599040 | tf_op jit(solution)/shard_map/all_gather | solution.py:87
  223.0 1.4 constant_dynamic-update-slice_fusion
  224.4 1.3 fusion.60
  225.7 1.3 fusion.69
  227.1 1.3 fusion.4
  228.3 1.9 fusion.5
  231.3 37.2 %all_gather.26 = bf16[2,64,1536]{1,0,2:T(2,128)(2,1)S(1)} all-gather(bf16[2,64,192]{1,0,2:T(2,128)(2,1)S(1)} %bitcast.93), channel_id=1, replica_groups=mesh['seq'=64,'tensor'=8] {'tensor'}, dimensions={2}, use_global_device_ids=true | all-gather | bytes 442368 | tf_op jit(solution)/shard_map/all_gather | solution.py:94
  269.9 1.0 convert_element_type.67
  271.4 1.1 multiply_convert_fusion.1
  272.6 1.9 collective-permute-start
  274.5 3.6 collective-permute-start.1
  278.2 1.4 fusion.43
  279.6 1.4 fusion.41
  281.0 1.4 fusion.45
  282.5 1.4 fusion.6
  283.9 1.4 fusion.9
  285.5 35.9 %all_gather.28 = bf16[2,64,1536]{1,0,2:T(2,128)(2,1)S(1)} all-gather(bf16[2,64,192]{1,0,2:T(2,128)(2,1)S(1)} %copy.45), channel_id=1, replica_groups=mesh['seq'=64,'tensor'=8] {'tensor'}, dimensions={2}, use_global_device_ids=true | all-gather | bytes 442368 | tf_op jit(solution)/shard_map/all_gather | solution.py:49
  322.6 34.9 %all_gather.30 = bf16[2,128,768]{1,0,2:T(2,128)(2,1)S(1)} all-gather(bf16[2,128,96]{1,0,2:T(2,128)(2,1)S(1)} %copy.50), channel_id=1, replica_groups=mesh['seq'=64,'tensor'=8] {'tensor'}, dimensions={2}, use_global_device_ids=true | all-gather | bytes 442368 | tf_op jit(solution)/shard_map/all_gather | solution.py:49
  358.8 1.9 multiply_reduce_fusion.1
  361.4 1.0 fusion.75
  363.9 1.1 reshape.68
  365.2 1.9 collective-permute-start.2
  367.4 1.6 copy.62
  368.9 3.6 collective-permute-start.3
  372.6 1.2 fusion.56
  373.8 1.2 fusion.10
  375.0 69.0 %reduce-scatter.9.cloned.1.call-done = bf16[192,128]{1,0:T(8,128)(2,1)} async-done(((bf16[1536,128]{1,0:T(8,128)(2,1)}), bf16[192,128]{1,0:T(8,128)(2,1)}) %reduce-scatter.9.cloned.1.call-update) | async-done | bytes 49168
  445.0 1.9 collective-permute-start.6
  447.0 2.6 collective-permute-start.7
  449.5 1.5 fusion.42
  451.1 1.5 fusion.40
  452.6 1.6 fusion.44
  454.2 1.6 fusion
  455.9 2.3 fusion.2
  459.4 99.1 %all-reduce.5.cloned.1.call-done = bf16[2,64,1536]{2,1,0:T(8,128)(2,1)} async-done(((bf16[2,64,1536]{2,1,0:T(8,128)(2,1)}), bf16[2,64,1536]{2,1,0:T(8,128)(2,1)}) %all-reduce.5.cloned.1.call-update) | async-done | bytes 393232 | tf_op jit(solution)/shard_map/psum | solution.py:70
  558.5 1.8 multiply_reduce_fusion
  560.3 1.1 fusion.77
  561.6 36.0 %all_gather.32 = bf16[2,64,1536]{1,0,2:T(2,128)(2,1)S(1)} all-gather(bf16[2,64,192]{1,0,2:T(2,128)(2,1)S(1)} %copy.60), channel_id=1, replica_groups=mesh['seq'=64,'tensor'=8] {'tensor'}, dimensions={2}, use_global_device_ids=true | all-gather | bytes 442368 | tf_op jit(solution)/shard_map/all_gather | solution.py:49
  597.6 1.1 convolution_convert_fusion.2
  (99 shorter events, 16.5 us)
Async XLA Ops:
  8.0 69.1 %copy-start = (bf16[2,64,192]{2,1,0:T(8,128)(2,1)S(1)}, bf16[2,64,192]{2,1,0:T(8,128)(2,1)}, u32[]{:S(2)}) copy-start(bf16[2,64,192]{2,1,0:T(8,128)(2,1)} %param.9) | copy-start | bytes 147460
  8.0 71.9 %copy-start.1 = (bf16[2,128,96]{1,2,0:T(8,128)(2,1)S(1)}, bf16[2,128,96]{1,2,0:T(8,128)(2,1)}, u32[]{:S(2)}) copy-start(bf16[2,128,96]{1,2,0:T(8,128)(2,1)} %param.17) | copy-start | bytes 147460
  8.0 80.3 %copy-start.15 = (bf16[24,2,96]{2,1,0:T(2,128)(2,1)S(1)}, bf16[24,2,96]{2,1,0:T(2,128)(2,1)}, u32[]{:S(2)}) copy-start(bf16[24,2,96]{2,1,0:T(2,128)(2,1)} %param.13) | copy-start | bytes 27652
  8.0 80.9 %copy-start.12 = (bf16[5,12,96]{2,1,0:T(8,128)(2,1)S(1)}, bf16[5,12,96]{2,1,0:T(8,128)(2,1)}, u32[]{:S(2)}) copy-start(bf16[5,12,96]{2,1,0:T(8,128)(2,1)} %param.16) | copy-start | bytes 34564
  8.0 222.3 %reduce-scatter.7.cloned.1.call-start = ((), (), s32[]{:S(2)}) async-start(), calls=%async_computation.5 | async-start | bytes 442368
  79.3 198.9 %all-gather.2.cloned.1.call-start = ((), (), s32[]{:S(2)}) async-start(), calls=%async_computation.2 | async-start | bytes 3993600 | tf_op jit(solution)/shard_map/all_gather | solution.py:99
  79.8 278.9 %all-reduce.3.cloned.1.call-start = ((), (), s32[]{:S(2)}) async-start(), calls=%async_computation.3 | async-start | bytes 786432 | tf_op jit(solution)/shard_map/psum | solution.py:70
  80.6 142.4 %collective-permute-start.4 = (bf16[2,2,96]{1,2,0:T(8,128)(2,1)}, bf16[2,2,96]{1,2,0:T(8,128)(2,1)}, u32[]{:S(2)}, u32[]{:S(2)}) collective-permute-start(bf16[2,2,96]{1,2,0:T(8,128)(2,1)} %get-tuple-element.28), channel_id=1, source_target_pairs={{8,0},{16,8},{24,16},{32,24},{40,32},{48,40},{56,48},{64,56},{72,6... | collective-permute-start | bytes 2312 | tf_op jit(solution)/shard_map/ppermute | solution.py:19
  85.6 138.8 %collective-permute-start.5 = (bf16[2,2,96]{1,2,0:T(8,128)(2,1)}, bf16[2,2,96]{1,2,0:T(8,128)(2,1)}, u32[]{:S(2)}, u32[]{:S(2)}) collective-permute-start(bf16[2,2,96]{1,2,0:T(8,128)(2,1)} %get-tuple-element.29), channel_id=1, source_target_pairs={{0,8},{8,16},{16,24},{24,32},{32,40},{40,48},{48,56},{56,64},{64,7... | collective-permute-start | bytes 2312 | tf_op jit(solution)/shard_map/ppermute | solution.py:18
  159.7 67.3 %copy-start.4 = (bf16[1,768,96]{1,2,0:T(8,128)(2,1)S(1)}, bf16[1,768,96]{1,2,0:T(8,128)(2,1)}, u32[]{:S(2)}) copy-start(bf16[1,768,96]{1,2,0:T(8,128)(2,1)} %copy.75) | copy-start | bytes 442372
  160.4 68.0 %copy-start.2 = (bf16[1,768,96]{1,2,0:T(8,128)(2,1)S(1)}, bf16[1,768,96]{1,2,0:T(8,128)(2,1)}, u32[]{:S(2)}) copy-start(bf16[1,768,96]{1,2,0:T(8,128)(2,1)} %copy.78) | copy-start | bytes 442372
  230.3 213.7 %reduce-scatter.9.cloned.1.call-start = ((), (), s32[]{:S(2)}) async-start(), calls=%async_computation.6 | async-start | bytes 442368
  269.9 4.6 copy-start.16
  270.9 0.5 copy-start.13
  271.4 12.5 %copy-start.9 = (bf16[2,64,192]{2,1,0:T(8,128)(2,1)S(1)}, bf16[2,64,192]{2,1,0:T(8,128)(2,1)}, u32[]{:S(2)}) copy-start(bf16[2,64,192]{2,1,0:T(8,128)(2,1)} %copy.67) | copy-start | bytes 147460
  272.6 7.0 %collective-permute-start = (bf16[2,2,1536]{2,1,0:T(2,128)(2,1)S(1)}, bf16[2,2,1536]{2,1,0:T(2,128)(2,1)S(1)}, u32[]{:S(2)}, u32[]{:S(2)}) collective-permute-start(bf16[2,2,1536]{2,1,0:T(2,128)(2,1)S(1)} %get-tuple-element.24), channel_id=1, source_target_pairs={{0,8},{8,16},{16,24},{24,32},{32,40},{40,48},{48,56},{56,64},{64,7... | collective-permute-start | bytes 36872 | tf_op jit(solution)/shard_map/ppermute | solution.py:18
  274.5 6.5 %collective-permute-start.1 = (bf16[2,2,1536]{2,1,0:T(2,128)(2,1)S(1)}, bf16[2,2,1536]{2,1,0:T(2,128)(2,1)S(1)}, u32[]{:S(2)}, u32[]{:S(2)}) collective-permute-start(bf16[2,2,1536]{2,1,0:T(2,128)(2,1)S(1)} %get-tuple-element.25), channel_id=1, source_target_pairs={{8,0},{16,8},{24,16},{32,24},{40,32},{48,40},{56,48},{64,56},{72,6... | collective-permute-start | bytes 36872 | tf_op jit(solution)/shard_map/ppermute | solution.py:19
  282.5 39.5 %copy-start.10 = (bf16[2,128,96]{1,2,0:T(8,128)(2,1)S(1)}, bf16[2,128,96]{1,2,0:T(8,128)(2,1)}, u32[]{:S(2)}) copy-start(bf16[2,128,96]{1,2,0:T(8,128)(2,1)} %param.14) | copy-start | bytes 147460
  322.0 0.6 copy-start.7
  358.2 0.6 copy-start.18
  362.5 0.6 copy-start.5
  365.1 193.4 %all-reduce.5.cloned.1.call-start = ((), (), s32[]{:S(2)}) async-start(), calls=%async_computation.4 | async-start | bytes 786432 | tf_op jit(solution)/shard_map/psum | solution.py:70
  365.2 7.4 %collective-permute-start.2 = (bf16[2,2,768]{2,1,0:T(2,128)(2,1)S(1)}, bf16[2,2,768]{2,1,0:T(2,128)(2,1)S(1)}, u32[]{:S(2)}, u32[]{:S(2)}) collective-permute-start(bf16[2,2,768]{2,1,0:T(2,128)(2,1)S(1)} %get-tuple-element.22), channel_id=1, source_target_pairs={{0,8},{8,16},{16,24},{24,32},{32,40},{40,48},{48,56},{56,64},{64,7... | collective-permute-start | bytes 18440 | tf_op jit(solution)/shard_map/ppermute | solution.py:18
  368.9 89.3 %collective-permute-start.3 = (bf16[2,2,768]{2,1,0:T(2,128)(2,1)S(1)}, bf16[2,2,768]{2,1,0:T(2,128)(2,1)S(1)}, u32[]{:S(2)}, u32[]{:S(2)}) collective-permute-start(bf16[2,2,768]{2,1,0:T(2,128)(2,1)S(1)} %get-tuple-element.23), channel_id=1, source_target_pairs={{8,0},{16,8},{24,16},{32,24},{40,32},{48,40},{56,48},{64,56},{72,6... | collective-permute-start | bytes 18440 | tf_op jit(solution)/shard_map/ppermute | solution.py:19
  445.0 6.1 collective-permute-start.6
  447.0 5.7 collective-permute-start.7
  452.6 5.6 copy-start.6
  454.2 4.3 copy-start.3
  454.2 4.3 copy-start.8
  454.2 104.3 %copy-start.11 = (f32[1536]{0:T(1024)S(1)}, f32[1536]{0:T(1024)}, u32[]{:S(2)}) copy-start(f32[1536]{0:T(1024)} %param.11) | copy-start | bytes 18436
  454.2 104.3 %copy-start.14 = (f32[2,64]{1,0:T(2,128)S(1)}, f32[2,64]{1,0:T(2,128)}, u32[]{:S(2)}) copy-start(f32[2,64]{1,0:T(2,128)} %copy-done.13) | copy-start | bytes 1540
  455.8 104.5 %copy-start.17 = (f32[2,64]{1,0:T(2,128)S(1)}, f32[2,64]{1,0:T(2,128)}, u32[]{:S(2)}) copy-start(f32[2,64]{1,0:T(2,128)} %copy-done.16) | copy-start | bytes 1540
Sparse Core Ops, SparseCore 0:
  79.4 80.6 reduce-scatter.6
  230.4 92.9 all-reduce.2
  365.2 78.7 reduce-scatter.8
  458.3 100.1 all-reduce.4
Sparse Core Ops, SparseCore 1:
  81.8 117.8 all-gather.1
where the time goes:
time: 607 us; the launch traced here: 606 us
  blocking collectives  341 us (56%)
  waiting for transfers between devices  169 us (28%)
  matrix products  27.6 us (5%)
  starting transfers between devices  22.8 us (4%)
  local copies, waits for them, and re-layouts  20.7 us (3%)
  between operations  15.9 us (3%)
  other arithmetic  9.67 us (2%)
    all_gather x3, blocking collectives, spread(): return lax.all_gather(field, 'tensor', axis=2, tiled=True)  107 us
    psum x2, waiting for transfers between devices, norm_back(): lax.psum(partial_grad.astype(jnp.bfloat16), 'tensor').astype(jnp.float32)  99.1 us
    unnamed x7, waiting for transfers between devices  69.6 us
    all_gather x1, blocking collectives, per_device(): lax.all_gather(w_out, 'seq', axis=1, tiled=True)  69.1 us
    all_gather x1, blocking collectives, per_device(): lax.all_gather(w_conv2, 'seq', axis=1, tiled=True)  65.4 us
    all_gather x1, blocking collectives, per_device(): lax.all_gather(w_up, 'seq', axis=0, tiled=True)  62.1 us
    all_gather x1, blocking collectives, per_device(): projected_full = lax.all_gather(projected, 'tensor', axis=2, tiled=True)  37.2 us
    dot_general x12, matrix products, matmul_back(): lax.dot_general(left, right, (((left.ndim - 1,), (right.ndim - 1,)), ((),...  15.9 us
  transfers between devices with their start and end apart: 13, of which 2 were waited for; matrix products, arithmetic and copies ran while one was open for 7% of the time, Pallas kernels for 0%

commit v1 on v0

--- a/solution.py
+++ b/solution.py
@@ -6,6 +6,7 @@
 C_COARSE = 1536
 C_FINE = 768
 EPS = 1e-06
+_attach_words = lambda slab_in: jnp.sum(lax.all_gather(slab_in, axis_name="tensor"), axis=0)
 
 
 def extended(shard, sides, width):
@@ -67,7 +68,7 @@
 def norm_back(partial_grad, field_full, gain, rank, part):
     field = field_full.astype(jnp.float32)
     start = rank * part
-    whole = lax.psum(partial_grad.astype(jnp.bfloat16), "tensor").astype(jnp.float32)
+    whole = _attach_words(partial_grad.astype(jnp.bfloat16)).astype(jnp.float32)
 
     def apply(value):
         return activate(value, gain)

time: 607 us -> 685 us (1.13)
  waiting for transfers between devices: 169 us -> 253 us
    all_gather x1, waiting for transfers between devices: 0.03 us -> 99.5 us  [per_device(): lax.all_gather(w_conv1, 'seq', axis=1, tiled=True)]
    psum x2 -> x0, waiting for transfers between devices: 99.1 us -> none  [norm_back(): lax.psum(partial_grad.astype(jnp.bfloat16), 'tensor').astype(jnp.float32)]
    all_gather x0 -> x2, waiting for transfers between devices: none -> 68.3 us  [lax.all_gather(slab_in, axis_name='tensor')]
    unnamed x7, waiting for transfers between devices: 69.6 us -> 84.4 us
    unnamed x56 -> x60, local copies, waits for them, and re-layouts: 15.2 us -> 11.7 us
  transfers between devices with their start and end apart: 13 -> 13, of which waited for: 2 -> 4; matrix products, arithmetic and copies ran while one was open for 7% -> 4% of each run, Pallas kernels for 0% -> 0%
where the time goes in v1:
time: 685 us; the launch traced here: 684 us
  blocking collectives  339 us (49%)
  waiting for transfers between devices  253 us (37%)
  matrix products  24.7 us (4%)
  starting transfers between devices  22.7 us (3%)
  local copies, waits for them, and re-layouts  18.5 us (3%)
  between operations  14.5 us (2%)
  other arithmetic  11 us (2%)
    all_gather x3, blocking collectives, spread(): return lax.all_gather(field, 'tensor', axis=2, tiled=True)  106 us
    all_gather x1, waiting for transfers between devices, per_device(): lax.all_gather(w_conv1, 'seq', axis=1, tiled=True)  99.5 us
    unnamed x7, waiting for transfers between devices  84.4 us
    all_gather x1, blocking collectives, per_device(): lax.all_gather(w_out, 'seq', axis=1, tiled=True)  69.1 us
    all_gather x2, waiting for transfers between devices, lax.all_gather(slab_in, axis_name='tensor')  68.3 us
    all_gather x1, blocking collectives, per_device(): lax.all_gather(w_conv2, 'seq', axis=1, tiled=True)  64.2 us
    all_gather x1, blocking collectives, per_device(): lax.all_gather(w_up, 'seq', axis=0, tiled=True)  63.3 us
    all_gather x1, blocking collectives, per_device(): projected_full = lax.all_gather(projected, 'tensor', axis=2, tiled=True)  36.7 us
  transfers between devices with their start and end apart: 13, of which 4 were waited for; matrix products, arithmetic and copies ran while one was open for 4% of the time, Pallas kernels for 0%

profile of v1, /device:TPU:32, one launch (start us, length us, event | category | flops | bytes accessed | tf_op | source)
XLA Modules:
  0.0 683.7 jit_solution(13342523825245579863)
XLA Ops:
  7.2 69.1 %all_gather.37 = bf16[192,1536]{0,1:T(8,128)(2,1)S(1)} all-gather(bf16[192,24]{0,1:T(8,128)(2,1)} %param.10), channel_id=1, replica_groups=mesh['seq'=64,'tensor'=8] {'seq'}, dimensions={1}, use_global_device_ids=true | all-gather | bytes 599040 | tf_op jit(solution)/shard_map/all_gather | solution.py:87
  77.3 1.1 reshape.68
  79.2 5.0 collective-permute-start.4
  84.2 1.9 collective-permute-start.5
  86.1 64.2 %all_gather.43 = bf16[5,768,96]{2,0,1:T(8,128)(2,1)S(1)} all-gather(bf16[5,12,96]{2,0,1:T(8,128)(2,1)S(1)} %copy.52), channel_id=1, replica_groups=mesh['seq'=64,'tensor'=8] {'seq'}, dimensions={1}, use_global_device_ids=true | all-gather | bytes 748800 | tf_op jit(solution)/shard_map/all_gather | solution.py:89
  150.3 2.1 fusion.107
  153.6 1.8 copy.76
  157.1 1.3 fusion.69
  158.8 1.3 fusion.4
  160.1 1.1 fusion.5
  162.8 63.3 %all_gather.41 = bf16[1536,2,96]{2,0,1:T(8,128)(2,1)S(1)} all-gather(bf16[24,2,96]{2,0,1:T(8,128)(2,1)S(1)} %copy.46), channel_id=1, replica_groups=mesh['seq'=64,'tensor'=8] {'seq'}, dimensions={0}, use_global_device_ids=true | all-gather | bytes 599040 | tf_op jit(solution)/shard_map/all_gather | solution.py:88
  226.4 0.9 reshape.69
  228.0 36.7 %all_gather.38 = bf16[2,64,1536]{1,0,2:T(2,128)(2,1)S(1)} all-gather(bf16[2,64,192]{1,0,2:T(2,128)(2,1)S(1)} %bitcast.98), channel_id=1, replica_groups=mesh['seq'=64,'tensor'=8] {'tensor'}, dimensions={2}, use_global_device_ids=true | all-gather | bytes 442368 | tf_op jit(solution)/shard_map/all_gather | solution.py:95
  265.4 1.1 multiply_convert_fusion.1
  267.1 1.9 collective-permute-start
  269.1 3.6 collective-permute-start.1
  272.8 2.4 reduce_sum.65
  275.2 99.5 %all-gather.6.cloned.1.call-done = bf16[5,1536,192]{2,1,0:T(8,128)(2,1)} async-done(((bf16[5,24,192]{2,1,0:T(8,128)(2,1)}), bf16[5,1536,192]{2,1,0:T(8,128)(2,1)}) %all-gather.6.cloned.1.call-update) | async-done | bytes 2949136 | tf_op jit(solution)/shard_map/all_gather | solution.py:100
  374.7 1.4 fusion.43
  376.2 1.4 fusion.41
  377.6 1.4 fusion.45
  379.0 1.4 fusion.6
  380.5 2.1 fusion.9
  382.6 1.0 copy.45
  383.5 35.5 %all_gather.40 = bf16[2,64,1536]{1,0,2:T(2,128)(2,1)S(1)} all-gather(bf16[2,64,192]{1,0,2:T(2,128)(2,1)S(1)} %copy.45), channel_id=1, replica_groups=mesh['seq'=64,'tensor'=8] {'tensor'}, dimensions={2}, use_global_device_ids=true | all-gather | bytes 442368 | tf_op jit(solution)/shard_map/all_gather | solution.py:50
  419.6 0.8 add_convert_fusion
  420.5 34.7 %all_gather.42 = bf16[2,128,768]{1,0,2:T(2,128)(2,1)S(1)} all-gather(bf16[2,128,96]{1,0,2:T(2,128)(2,1)S(1)} %copy.50), channel_id=1, replica_groups=mesh['seq'=64,'tensor'=8] {'tensor'}, dimensions={2}, use_global_device_ids=true | all-gather | bytes 442368 | tf_op jit(solution)/shard_map/all_gather | solution.py:50
  455.8 1.6 multiply_reduce_fusion.1
  457.4 1.1 fusion.75
  460.0 1.1 reshape.70
  461.1 83.6 %reduce-scatter.9.cloned.1.call-done = bf16[192,128]{1,0:T(8,128)(2,1)} async-done(((bf16[1536,128]{1,0:T(8,128)(2,1)}), bf16[192,128]{1,0:T(8,128)(2,1)}) %reduce-scatter.9.cloned.1.call-update) | async-done | bytes 49168
  544.8 0.9 reshape.71
  545.8 1.9 collective-permute-start.6
  547.7 2.6 collective-permute-start.7
  550.3 1.5 fusion.42
  551.8 1.5 fusion.40
  553.4 1.5 fusion.44
  554.9 1.6 fusion
  556.6 2.3 fusion.2
  559.0 3.1 collective-permute-start.2
  563.2 2.4 collective-permute-start.3
  565.9 1.0 collective-permute-done.3
  567.6 0.9 fusion.13
  568.5 68.3 %all-gather.10.cloned.1.call-done = bf16[16,64,1536]{2,1,0:T(8,128)(2,1)} async-done(((bf16[2,64,1536]{2,1,0:T(8,128)(2,1)}), bf16[16,64,1536]{2,1,0:T(8,128)(2,1)}) %all-gather.10.cloned.1.call-update) | async-done | bytes 3145744 | tf_op jit(solution)/shard_map/all_gather | solution.py:9
  636.8 2.4 reduce_sum.80
  639.2 1.0 multiply_reduce_fusion
  640.5 35.6 %all_gather.48 = bf16[2,64,1536]{1,0,2:T(2,128)(2,1)S(1)} all-gather(bf16[2,64,192]{1,0,2:T(2,128)(2,1)S(1)} %copy.60), channel_id=1, replica_groups=mesh['seq'=64,'tensor'=8] {'tensor'}, dimensions={2}, use_global_device_ids=true | all-gather | bytes 442368 | tf_op jit(solution)/shard_map/all_gather | solution.py:50
  676.1 1.1 convolution_convert_fusion.2
  (105 shorter events, 14.1 us)
Async XLA Ops:
  7.2 69.1 %copy-start = (bf16[2,64,192]{2,1,0:T(8,128)(2,1)S(1)}, bf16[2,64,192]{2,1,0:T(8,128)(2,1)}, u32[]{:S(2)}) copy-start(bf16[2,64,192]{2,1,0:T(8,128)(2,1)} %param.9) | copy-start | bytes 147460
  7.2 71.3 %copy-start.1 = (bf16[2,128,96]{1,2,0:T(8,128)(2,1)S(1)}, bf16[2,128,96]{1,2,0:T(8,128)(2,1)}, u32[]{:S(2)}) copy-start(bf16[2,128,96]{1,2,0:T(8,128)(2,1)} %param.17) | copy-start | bytes 147460
  7.2 78.9 %copy-start.15 = (bf16[5,12,96]{2,1,0:T(8,128)(2,1)S(1)}, bf16[5,12,96]{2,1,0:T(8,128)(2,1)}, u32[]{:S(2)}) copy-start(bf16[5,12,96]{2,1,0:T(8,128)(2,1)} %param.16) | copy-start | bytes 34564
  7.2 219.2 %reduce-scatter.7.cloned.1.call-start = ((), (), s32[]{:S(2)}) async-start(), calls=%async_computation.5 | async-start | bytes 442368
  78.4 194.3 %all-gather.8.cloned.1.call-start = ((), (), s32[]{:S(2)}) async-start(), calls=%async_computation.3 | async-start | bytes 3538944 | tf_op jit(solution)/shard_map/all_gather | solution.py:9
  79.2 77.3 %collective-permute-start.4 = (bf16[2,2,96]{1,2,0:T(8,128)(2,1)}, bf16[2,2,96]{1,2,0:T(8,128)(2,1)S(1)}, u32[]{:S(2)}, u32[]{:S(2)}) collective-permute-start(bf16[2,2,96]{1,2,0:T(8,128)(2,1)} %get-tuple-element.28), channel_id=1, source_target_pairs={{8,0},{16,8},{24,16},{32,24},{40,32},{48,40},{56,48},{64,56},{72,6... | collective-permute-start | bytes 2312 | tf_op jit(solution)/shard_map/ppermute | solution.py:20
  84.2 74.3 %collective-permute-start.5 = (bf16[2,2,96]{1,2,0:T(8,128)(2,1)}, bf16[2,2,96]{1,2,0:T(8,128)(2,1)S(1)}, u32[]{:S(2)}, u32[]{:S(2)}) collective-permute-start(bf16[2,2,96]{1,2,0:T(8,128)(2,1)} %get-tuple-element.29), channel_id=1, source_target_pairs={{0,8},{8,16},{16,24},{24,32},{32,40},{40,48},{48,56},{56,64},{64,7... | collective-permute-start | bytes 2312 | tf_op jit(solution)/shard_map/ppermute | solution.py:19
  155.8 5.5 copy-start.2
  156.1 5.9 copy-start.8
  156.1 6.7 copy-start.18
  156.4 69.6 %copy-start.4 = (bf16[1,768,96]{1,2,0:T(8,128)(2,1)}, bf16[1,768,96]{1,2,0:T(8,128)(2,1)S(1)}, u32[]{:S(2)}) copy-start(bf16[1,768,96]{1,2,0:T(8,128)(2,1)S(1)} %copy.78) | copy-start | bytes 442372
  161.3 213.5 %all-gather.6.cloned.1.call-start = ((), (), s32[]{:S(2)}) async-start(), calls=%async_computation.2 | async-start | bytes 3993600 | tf_op jit(solution)/shard_map/all_gather | solution.py:100
  162.0 382.8 %reduce-scatter.9.cloned.1.call-start = ((), (), s32[]{:S(2)}) async-start(), calls=%async_computation.6 | async-start | bytes 442368
  265.4 7.3 %copy-start.19 = (f32[2,64]{1,0:T(2,128)}, f32[2,64]{1,0:T(2,128)S(1)}, u32[]{:S(2)}) copy-start(f32[2,64]{1,0:T(2,128)S(1)} %multiply_reduce_fusion.3) | copy-start | bytes 1540
  265.4 7.3 %copy-start.16 = (f32[2,64]{1,0:T(2,128)}, f32[2,64]{1,0:T(2,128)S(1)}, u32[]{:S(2)}) copy-start(f32[2,64]{1,0:T(2,128)S(1)} %fusion.89) | copy-start | bytes 1540
  267.1 109.0 %collective-permute-start = (bf16[2,2,1536]{2,1,0:T(2,128)(2,1)}, bf16[2,2,1536]{2,1,0:T(2,128)(2,1)}, u32[]{:S(2)}, u32[]{:S(2)}) collective-permute-start(bf16[2,2,1536]{2,1,0:T(2,128)(2,1)} %get-tuple-element.24), channel_id=1, source_target_pairs={{0,8},{8,16},{16,24},{24,32},{32,40},{40,48},{48,56},{56,64},{64,7... | collective-permute-start | bytes 36872 | tf_op jit(solution)/shard_map/ppermute | solution.py:19
  269.1 108.5 %collective-permute-start.1 = (bf16[2,2,1536]{2,1,0:T(2,128)(2,1)}, bf16[2,2,1536]{2,1,0:T(2,128)(2,1)}, u32[]{:S(2)}, u32[]{:S(2)}) collective-permute-start(bf16[2,2,1536]{2,1,0:T(2,128)(2,1)} %get-tuple-element.25), channel_id=1, source_target_pairs={{8,0},{16,8},{24,16},{32,24},{40,32},{48,40},{56,48},{64,56},{72,6... | collective-permute-start | bytes 36872 | tf_op jit(solution)/shard_map/ppermute | solution.py:20
  374.7 5.8 copy-start.13
  420.4 35.4 %copy-start.11 = (bf16[2,128,96]{1,2,0:T(8,128)(2,1)}, bf16[2,128,96]{1,2,0:T(8,128)(2,1)S(1)}, u32[]{:S(2)}) copy-start(bf16[2,128,96]{1,2,0:T(8,128)(2,1)S(1)} %add_convert_fusion) | copy-start | bytes 147460
  458.5 0.6 copy-start.6
  461.1 175.7 %all-gather.10.cloned.1.call-start = ((), (), s32[]{:S(2)}) async-start(), calls=%async_computation.4 | async-start | bytes 3538944 | tf_op jit(solution)/shard_map/all_gather | solution.py:9
  545.8 6.1 collective-permute-start.6
  547.7 5.7 collective-permute-start.7
  554.9 7.5 %copy-start.7 = (bf16[2,128,96]{2,1,0:T(8,128)(2,1)S(1)}, bf16[2,128,96]{2,1,0:T(8,128)(2,1)}, u32[]{:S(2)}) copy-start(bf16[2,128,96]{2,1,0:T(8,128)(2,1)} %copy-done.6) | copy-start | bytes 147460
  554.9 10.7 %copy-start.10 = (bf16[1,768,96]{1,2,0:T(8,128)(2,1)S(1)}, bf16[1,768,96]{1,2,0:T(8,128)(2,1)}, u32[]{:S(2)}) copy-start(bf16[1,768,96]{1,2,0:T(8,128)(2,1)} %copy.76) | copy-start | bytes 442372
  554.9 12.0 %copy-start.9 = (bf16[1,768,96]{1,2,0:T(8,128)(2,1)S(1)}, bf16[1,768,96]{1,2,0:T(8,128)(2,1)}, u32[]{:S(2)}) copy-start(bf16[1,768,96]{1,2,0:T(8,128)(2,1)} %copy-done.8) | copy-start | bytes 442372
  556.5 10.7 %copy-start.3 = (bf16[1,768,96]{1,2,0:T(8,128)(2,1)S(1)}, bf16[1,768,96]{1,2,0:T(8,128)(2,1)}, u32[]{:S(2)}) copy-start(bf16[1,768,96]{1,2,0:T(8,128)(2,1)} %copy-done.2) | copy-start | bytes 442372
  556.5 11.0 %copy-start.5 = (bf16[1,768,96]{1,2,0:T(8,128)(2,1)S(1)}, bf16[1,768,96]{1,2,0:T(8,128)(2,1)}, u32[]{:S(2)}) copy-start(bf16[1,768,96]{1,2,0:T(8,128)(2,1)} %copy-done.4) | copy-start | bytes 442372
  556.5 11.0 %copy-start.12 = (bf16[2,128,96]{1,2,0:T(8,128)(2,1)S(1)}, bf16[2,128,96]{1,2,0:T(8,128)(2,1)}, u32[]{:S(2)}) copy-start(bf16[2,128,96]{1,2,0:T(8,128)(2,1)} %copy-done.11) | copy-start | bytes 147460
  559.0 6.6 collective-permute-start.2
  562.4 76.8 %copy-start.14 = (f32[1536]{0:T(1024)S(1)}, f32[1536]{0:T(1024)}, u32[]{:S(2)}) copy-start(f32[1536]{0:T(1024)} %param.11) | copy-start | bytes 18436
  562.4 76.8 %copy-start.17 = (f32[2,64]{1,0:T(2,128)S(1)}, f32[2,64]{1,0:T(2,128)}, u32[]{:S(2)}) copy-start(f32[2,64]{1,0:T(2,128)} %copy-done.16) | copy-start | bytes 1540
  563.2 3.8 collective-permute-start.3
  567.2 73.0 %copy-start.20 = (f32[2,64]{1,0:T(2,128)S(1)}, f32[2,64]{1,0:T(2,128)}, u32[]{:S(2)}) copy-start(f32[2,64]{1,0:T(2,128)} %copy-done.19) | copy-start | bytes 1540
Sparse Core Ops, SparseCore 0:
  78.5 80.6 reduce-scatter.6
  162.4 78.1 all-gather.7
  242.7 131.9 all-gather.5
  461.2 83.4 reduce-scatter.8
  559.0 77.7 all-gather.9
